TPU v7x, 32 devices: a whole 2x2x4 slice. The times are simulated.
32 devices in a mesh: dp: 8 (over z, x), grp: 4 (over y, core).
Axes of the slice: x: 2, y: 2, z: 4, core: 2. Of those that a mesh axis runs over, the one named last changes fastest.
Arguments:
- down_in: bfloat16 [96, 32, 32, 160], P(('dp', 'grp')), may hold values from -6 to 6
- right_in: bfloat16 [96, 32, 32, 160], P(('dp', 'grp')), may hold values from -6 to 6
- pixel_mask: int32 [96, 32, 32], P(('dp', 'grp')), may hold values 0 or 1
- down_cot: bfloat16 [96, 32, 32, 160], P(('dp', 'grp')), may hold values from -6 to 6
- right_cot: bfloat16 [96, 32, 32, 160], P(('dp', 'grp')), may hold values from -6 to 6
- v_down1: bfloat16 [2, 1920, 160], P(None, 'dp'), may hold values from -0.125 to 0.125
- v_down2: bfloat16 [2, 1920, 320], P(None, 'dp'), may hold values from -0.125 to 0.125
- v_right1: bfloat16 [2, 1280, 160], P(None, 'dp'), may hold values from -0.15625 to 0.15625
- v_skip: bfloat16 [2, 320, 160], P(None, 'dp'), may hold values from -0.3125 to 0.3125
- v_right2: bfloat16 [2, 1280, 320], P(None, 'dp'), may hold values from -0.15625 to 0.15625
- gains: float32 [2, 1120], replicated, may hold values from 0.1 to 1.9
- biases: float32 [2, 1120], replicated, may hold values from -0.5 to 0.5
Outputs:
- down_out: bfloat16 [96, 32, 32, 160], P(('dp', 'grp'))
- right_out: bfloat16 [96, 32, 32, 160], P(('dp', 'grp'))
- down_grad: float32 [96, 32, 32, 160], P(('dp', 'grp'))
- right_grad: float32 [96, 32, 32, 160], P(('dp', 'grp'))
- grad_down1: float32 [2, 1920, 160], P(None, 'dp')
- grad_down2: float32 [2, 1920, 320], P(None, 'dp')
- grad_right1: float32 [2, 1280, 160], P(None, 'dp')
- grad_skip: float32 [2, 320, 160], P(None, 'dp')
- grad_right2: float32 [2, 1280, 320], P(None, 'dp')
- grad_gains: float32 [2, 1120], replicated
- grad_biases: float32 [2, 1120], replicated
Inputs may be any that keep to these rules, and one draw needn't show every extreme that they name: `pixel_mask`: 1 marks a counted pixel, 0 one that is not.
All inputs are finite; a program needn't handle non-finite values. No bound on the sum of `pixel_mask` on one device may be relied on, other than what follows from the above.
Results may differ from a plain program's by a relative error of at most 0.015.
Values may be sent and summed in bfloat16 or wider, within the bound.
A program may use at most 256 MiB of HBM per device.

v0:
```python
import jax
import jax.numpy as jnp
from jax import lax
from jax.sharding import PartitionSpec as P

LAYERS = 2


def span_list(filters):
    return [
        (0, filters),
        (filters, 3 * filters),
        (3 * filters, 4 * filters),
        (4 * filters, 5 * filters),
        (5 * filters, 7 * filters),
    ]


def tap_offsets(stencil):
    if stencil == "down":
        return [(row_off, col_off) for row_off in range(2) for col_off in range(3)]
    return [(row_off, col_off) for row_off in range(2) for col_off in range(2)]


def side_pad(stencil):
    return 2 if stencil == "down" else 1


def padded_cells(cells, stencil):
    return jnp.pad(cells, ((0, 0), (1, 0), (1, side_pad(stencil) - 1), (0, 0)))


def conv_apply(cells, weight, stencil):
    height, breadth, channels = (cells.shape[1], cells.shape[2], cells.shape[3])
    padded = padded_cells(cells, stencil)
    summed = None
    for tap_num, (row_off, col_off) in enumerate(tap_offsets(stencil)):
        window = padded[:, row_off : row_off + height, col_off : col_off + breadth, :]
        weight_tap = weight[tap_num * channels : (tap_num + 1) * channels]
        contrib = jnp.einsum(
            "bhwc,co->bhwo", window, weight_tap, preferred_element_type=jnp.float32
        )
        summed = contrib if summed is None else summed + contrib
    return summed


def conv_input_grad(grad_out, weight, stencil):
    breadth = grad_out.shape[2]
    offsets = tap_offsets(stencil)
    channels = weight.shape[0] // len(offsets)
    summed = None
    for tap_num, (row_off, col_off) in enumerate(offsets):
        weight_tap = weight[tap_num * channels : (tap_num + 1) * channels]
        contrib = jnp.einsum(
            "bhwo,co->bhwc", grad_out, weight_tap, preferred_element_type=jnp.float32
        )
        placed = jnp.pad(
            contrib,
            ((0, 0), (row_off, 1 - row_off), (col_off, side_pad(stencil) - col_off), (0, 0)),
        )
        summed = placed if summed is None else summed + placed
    return summed[:, 1:, 1 : 1 + breadth, :]


def conv_weight_grad(cells, grad_out, stencil):
    height, breadth = (cells.shape[1], cells.shape[2])
    padded = padded_cells(cells, stencil)
    pieces = []
    for row_off, col_off in tap_offsets(stencil):
        window = padded[:, row_off : row_off + height, col_off : col_off + breadth, :]
        pieces.append(
            jnp.einsum("bhwc,bhwo->co", window, grad_out, preferred_element_type=jnp.float32)
        )
    return jnp.concatenate(pieces, axis=0)


def pair_elu(values):
    return jax.nn.elu(jnp.concatenate([values, -values], axis=-1))


def elu_back(grad, source):
    channels = source.shape[-1]
    upper = jnp.where(source > 0, 1.0, jnp.exp(source))
    lower = jnp.where(source < 0, 1.0, jnp.exp(-source))
    return grad[..., :channels] * upper - grad[..., channels:] * lower


def gate_apply(flow, gate):
    channels = flow.shape[-1]
    return flow + gate[..., :channels] * jax.nn.sigmoid(gate[..., channels:])


def gate_back(grad, gate):
    channels = grad.shape[-1]
    top_half = gate[..., :channels]
    squash = jax.nn.sigmoid(gate[..., channels:])
    return jnp.concatenate(
        [grad * squash, grad * top_half * squash * (1.0 - squash)], axis=-1
    ).astype(jnp.bfloat16)


def prepare(whole, gains, spans):
    scaled = []
    inverse = []
    for full, (start_col, stop_col) in zip(whole, spans):
        values = full.astype(jnp.float32)
        recip = lax.rsqrt(jnp.sum(values * values, axis=1))
        scaled.append(
            (values * (gains[:, start_col:stop_col] * recip)[:, None, :]).astype(jnp.bfloat16)
        )
        inverse.append(recip)
    return (scaled, inverse)


def column_sum(grad):
    return jnp.sum(grad, axis=(0, 1, 2), dtype=jnp.float32)


def on_device(
    down_in,
    right_in,
    pixel_mask,
    down_cot,
    right_cot,
    v_down1,
    v_down2,
    v_right1,
    v_skip,
    v_right2,
    gains,
    biases,
):
    filters = down_in.shape[-1]
    spans = span_list(filters)
    shards = (v_down1, v_down2, v_right1, v_skip, v_right2)
    whole = (
        lax.all_gather(v_down1, "dp", axis=1, tiled=True),
        lax.all_gather(v_down2, "dp", axis=1, tiled=True),
        lax.all_gather(v_right1, "dp", axis=1, tiled=True),
        lax.all_gather(v_skip, "dp", axis=1, tiled=True),
        lax.all_gather(v_right2, "dp", axis=1, tiled=True),
    )
    scaled, inverse = prepare(whole, gains, spans)
    down_flow = down_in.astype(jnp.float32)
    right_flow = right_in.astype(jnp.float32)
    activated = pair_elu(down_flow).astype(jnp.bfloat16)
    kept = []
    for layer_num in range(LAYERS):
        weights = [scaled_now[layer_num] for scaled_now in scaled]
        bias_parts = [biases[layer_num, start_col:stop_col] for start_col, stop_col in spans]
        hidden_down = conv_apply(activated, weights[0], "down") + bias_parts[0]
        act_down = pair_elu(hidden_down).astype(jnp.bfloat16)
        gate_down = conv_apply(act_down, weights[1], "down") + bias_parts[1]
        new_down = gate_apply(down_flow, gate_down)
        new_act = pair_elu(new_down).astype(jnp.bfloat16)
        act_right = pair_elu(right_flow).astype(jnp.bfloat16)
        skip_term = jnp.einsum(
            "bhwk,ko->bhwo", new_act, weights[3], preferred_element_type=jnp.float32
        )
        hidden_right = (
            conv_apply(act_right, weights[2], "right") + skip_term + bias_parts[2] + bias_parts[3]
        )
        act_hidden = pair_elu(hidden_right).astype(jnp.bfloat16)
        gate_right = conv_apply(act_hidden, weights[4], "right") + bias_parts[4]
        new_right = gate_apply(right_flow, gate_right)
        kept.append(
            (
                down_flow,
                activated,
                hidden_down,
                act_down,
                gate_down,
                new_down,
                new_act,
                right_flow,
                act_right,
                hidden_right,
                act_hidden,
                gate_right,
            )
        )
        down_flow, right_flow, activated = (new_down, new_right, new_act)
    down_out = down_flow.astype(jnp.bfloat16)
    right_out = right_flow.astype(jnp.bfloat16)
    whole = (
        lax.all_gather(v_down1, "dp", axis=1, tiled=True),
        lax.all_gather(v_down2, "dp", axis=1, tiled=True),
        lax.all_gather(v_right1, "dp", axis=1, tiled=True),
        lax.all_gather(v_skip, "dp", axis=1, tiled=True),
        lax.all_gather(v_right2, "dp", axis=1, tiled=True),
    )
    scaled, inverse = prepare(whole, gains, spans)
    mask_float = pixel_mask.astype(jnp.float32)[..., None]
    grad_down = down_cot.astype(jnp.float32) * mask_float
    grad_right = right_cot.astype(jnp.float32) * mask_float
    grad_cells = jnp.zeros(grad_down.shape[:-1] + (2 * filters,), jnp.float32)
    layer_grads = [None] * LAYERS
    layer_bias = [None] * LAYERS
    for layer_num in reversed(range(LAYERS)):
        (
            down_flow,
            activated,
            hidden_down,
            act_down,
            gate_down,
            new_down,
            new_act,
            right_flow,
            act_right,
            hidden_right,
            act_hidden,
            gate_right,
        ) = kept[layer_num]
        weights = [scaled_now[layer_num] for scaled_now in scaled]
        grad_gate_right = gate_back(grad_right, gate_right)
        grad_w_right2 = conv_weight_grad(act_hidden, grad_gate_right, "right")
        grad_hid_right = elu_back(
            conv_input_grad(grad_gate_right, weights[4], "right"), hidden_right
        ).astype(jnp.bfloat16)
        grad_w_right1 = conv_weight_grad(act_right, grad_hid_right, "right")
        grad_w_skip = jnp.einsum(
            "bhwc,bhwo->co", new_act, grad_hid_right, preferred_element_type=jnp.float32
        )
        grad_cells = grad_cells + jnp.einsum(
            "bhwo,co->bhwc", grad_hid_right, weights[3], preferred_element_type=jnp.float32
        )
        grad_right = grad_right + elu_back(
            conv_input_grad(grad_hid_right, weights[2], "right"), right_flow
        )
        grad_down = grad_down + elu_back(grad_cells, new_down)
        grad_gate_down = gate_back(grad_down, gate_down)
        grad_w_down2 = conv_weight_grad(act_down, grad_gate_down, "down")
        grad_hid_down = elu_back(
            conv_input_grad(grad_gate_down, weights[1], "down"), hidden_down
        ).astype(jnp.bfloat16)
        grad_w_down1 = conv_weight_grad(activated, grad_hid_down, "down")
        grad_cells = conv_input_grad(grad_hid_down, weights[0], "down")
        layer_grads[layer_num] = (
            grad_w_down1,
            grad_w_down2,
            grad_w_right1,
            grad_w_skip,
            grad_w_right2,
        )
        right_bias = column_sum(grad_hid_right)
        layer_bias[layer_num] = jnp.concatenate(
            [
                column_sum(grad_hid_down),
                column_sum(grad_gate_down),
                right_bias,
                right_bias,
                column_sum(grad_gate_right),
            ]
        )
    down_grad = grad_down + elu_back(grad_cells, kept[0][0])
    local_grads = [
        jnp.stack([layer_grads[layer_num][map_num] for layer_num in range(LAYERS)])
        for map_num in range(5)
    ]
    bias_local = jnp.stack(layer_bias)
    row_sums = (
        lax.psum_scatter(local_grads[0], "dp", scatter_dimension=1, tiled=True),
        lax.psum_scatter(local_grads[1], "dp", scatter_dimension=1, tiled=True),
        lax.psum_scatter(local_grads[2], "dp", scatter_dimension=1, tiled=True),
        lax.psum_scatter(local_grads[3], "dp", scatter_dimension=1, tiled=True),
        lax.psum_scatter(local_grads[4], "dp", scatter_dimension=1, tiled=True),
    )
    group_sums = (
        lax.psum(row_sums[0].astype(jnp.bfloat16), "grp").astype(jnp.float32),
        lax.psum(row_sums[1].astype(jnp.bfloat16), "grp").astype(jnp.float32),
        lax.psum(row_sums[2].astype(jnp.bfloat16), "grp").astype(jnp.float32),
        lax.psum(row_sums[3].astype(jnp.bfloat16), "grp").astype(jnp.float32),
        lax.psum(row_sums[4].astype(jnp.bfloat16), "grp").astype(jnp.float32),
    )
    units = [
        shards[map_num].astype(jnp.float32) * inverse[map_num][:, None, :] for map_num in range(5)
    ]
    bias_sum = lax.psum(bias_local, ("dp", "grp"))
    dots_shard = jnp.concatenate(
        [jnp.sum(units[map_num] * group_sums[map_num], axis=1) for map_num in range(5)], axis=1
    )
    gain_sum = lax.psum(dots_shard, "dp")
    grad_dirs = []
    for map_num, (start_col, stop_col) in enumerate(spans):
        factor = (gains[:, start_col:stop_col] * inverse[map_num])[:, None, :]
        grad_dirs.append(
            factor * (group_sums[map_num] - units[map_num] * gain_sum[:, None, start_col:stop_col])
        )
    return (
        down_out,
        right_out,
        down_grad,
        grad_right,
        grad_dirs[0],
        grad_dirs[1],
        grad_dirs[2],
        grad_dirs[3],
        grad_dirs[4],
        gain_sum,
        bias_sum,
    )


def solution(mesh):
    placed = (
        P(("dp", "grp"), None, None, None),
        P(("dp", "grp"), None, None, None),
        P(("dp", "grp"), None, None),
        P(("dp", "grp"), None, None, None),
        P(("dp", "grp"), None, None, None),
        P(None, "dp", None),
        P(None, "dp", None),
        P(None, "dp", None),
        P(None, "dp", None),
        P(None, "dp", None),
        P(),
        P(),
    )
    return jax.shard_map(
        on_device,
        mesh=mesh,
        in_specs=placed,
        out_specs=(
            P(("dp", "grp"), None, None, None),
            P(("dp", "grp"), None, None, None),
            P(("dp", "grp"), None, None, None),
            P(("dp", "grp"), None, None, None),
            P(None, "dp", None),
            P(None, "dp", None),
            P(None, "dp", None),
            P(None, "dp", None),
            P(None, "dp", None),
            P(),
            P(),
        ),
        check_vma=False,
    )
```

profile of v0, /device:TPU:0, one launch (start us, length us, event | category | flops | bytes accessed | tf_op | source)
XLA Modules:
  0.0 1093.7 jit_solution(6300883025291663017)
XLA Ops:
  24.0 33.5 %all_gather.23 = bf16[2,320,160]{2,0,1:T(2,128)(2,1)S(1)} all-gather(bf16[2,40,160]{2,0,1:T(2,128)(2,1)S(1)} %copy.37), channel_id=1, replica_groups=mesh['dp'=8,'grp'=4] {'dp'}, dimensions={1}, use_global_device_ids=true | all-gather | bytes 230400 | tf_op jit(solution)/shard_map/all_gather | solution.py:140
  57.9 36.9 %all_gather.22 = bf16[2,1280,160]{2,0,1:T(2,128)(2,1)S(1)} all-gather(bf16[2,160,160]{2,0,1:T(2,128)(2,1)S(1)} %copy.35), channel_id=1, replica_groups=mesh['dp'=8,'grp'=4] {'dp'}, dimensions={1}, use_global_device_ids=true | all-gather | bytes 921600 | tf_op jit(solution)/shard_map/all_gather | solution.py:139
  97.0 5.3 fusion.3
  105.7 6.1 copy.33
  140.7 40.0 %all-gather.6.cloned.1.call-done = bf16[2,1920,320]{2,1,0:T(8,128)(2,1)} async-done(((bf16[2,240,320]{2,1,0:T(8,128)(2,1)}), bf16[2,1920,320]{2,1,0:T(8,128)(2,1)}) %all-gather.6.cloned.1.call-update) | async-done | bytes 2457616 | tf_op jit(solution)/shard_map/all_gather | solution.py:138
  186.1 3.8 fusion.73
  189.9 3.8 fusion.75
  193.7 3.7 fusion.168
  197.4 3.9 fusion.69
  201.3 7.9 add_add_fusion.3
  223.7 5.4 fusion.292
  233.2 3.7 fusion.89
  237.0 3.8 fusion.91
  244.4 3.8 fusion.175
  248.2 3.8 fusion.87
  252.0 4.3 fusion.293
  267.7 4.9 add_add_fusion.1
  288.1 9.1 add_add_fusion.2
  300.4 11.1 %convert_reduce_fusion.11 = (u32[3,32,160]{2,1,0:T(8,128)}, u32[3,32,160]{2,1,0:T(8,128)}, f32[3,32,32,160]{3,2,1,0:T(8,128)S(1)}) fusion(f32[160]{0:T(256)S(1)} %bitcast.665, f32[160]{0:T(256)S(1)} %bitcast.664, bf16[2,320,160]{1,2,0:T(8,128)(2,1)S(1)} %fusion.156, f32[3,32,32,160]{3,2,1,0:T(8,128)} %get-tuple-element.73, ...), kind=kOutput, calls=%fused_computation.101 | convolution fusion | flops 326338560 | bytes 15190016 | tf_op jit(solution)/shard_map/bhwk,ko->bhwo/dot_general | solution.py:157
  322.7 4.7 multiply_convert_fusion.7
  329.1 3.8 fusion.184
  332.9 3.8 fusion.183
  336.7 3.7 fusion.182
  340.4 3.7 fusion.181
  344.2 11.0 %pad_add_fusion.6 = f32[3,33,33,320]{3,2,1,0:T(8,128)} fusion(f32[3,32,32,320]{3,2,1,0:T(8,128)} %fusion.184, f32[3,32,32,320]{3,2,1,0:T(8,128)} %fusion.183, f32[3,32,32,320]{3,2,1,0:T(8,128)} %fusion.182, f32[3,32,32,320]{3,2,1,0:T(8,128)} %fusion.181), kind=kLoop, calls=%fused_computation.26 | loop fusion | flops 3136320 | bytes 19910400 | tf_op jit(solution)/shard_map/add | solution.py:61
  355.2 6.4 convert_reduce_fusion.12
  383.7 11.1 %pad_add_fusion.4 = f32[3,33,33,320]{3,2,1,0:T(8,128)} fusion(f32[3,32,32,320]{3,2,1,0:T(8,128)} %fusion.207, f32[3,32,32,320]{3,2,1,0:T(8,128)} %fusion.206, f32[3,32,32,320]{3,2,1,0:T(8,128)} %fusion.205, f32[3,32,32,320]{3,2,1,0:T(8,128)} %fusion.204), kind=kLoop, calls=%fused_computation.24 | loop fusion | flops 3136320 | bytes 19910400 | tf_op jit(solution)/shard_map/add | solution.py:61
  394.8 14.6 %multiply_convert_fusion.3 = (bf16[3,32,32,160]{3,2,1,0:T(8,128)(2,1)S(1)}, f32[3,32,32,160]{3,2,1,0:T(8,128)S(1)}, bf16[3,32,32,160]{3,2,1,0:T(8,128)(2,1)}, bf...) fusion(f32[3,32,32,320]{3,2,1,0:T(8,128)} %copy-done.24, f32[3,32,32,160]{3,2,1,0:T(8,128)} %copy-done.39, ...), kind=kLoop, calls=%fused_computation.155 | loop fusion | flops 16220160 | bytes 24588288 | tf_op jit(solution)/shard_map/convert.2
  425.8 3.8 fusion.178
  429.6 3.8 fusion.177
  433.4 11.0 %pad_add_fusion.3 = f32[3,33,33,320]{3,2,1,0:T(8,128)} fusion(f32[3,32,32,320]{3,2,1,0:T(8,128)} %fusion.180, f32[3,32,32,320]{3,2,1,0:T(8,128)} %fusion.179, f32[3,32,32,320]{3,2,1,0:T(8,128)} %fusion.178, f32[3,32,32,320]{3,2,1,0:T(8,128)} %fusion.177), kind=kLoop, calls=%fused_computation.23 | loop fusion | flops 3136320 | bytes 19910400 | tf_op jit(solution)/shard_map/add | solution.py:61
  444.5 6.5 convert_reduce_fusion.14
  460.6 3.7 fusion.173
  468.0 3.7 fusion.171
  471.7 4.0 fusion.170
  475.7 8.8 pad_add_fusion.5
  514.3 12.8 %fusion.20 = f32[3,32,32,320]{3,2,1,0:T(8,128)} fusion(f32[3,32,32,320]{3,2,1,0:T(8,128)} %fusion.198, f32[3,32,32,320]{3,2,1,0:T(8,128)} %fusion.196, f32[3,32,32,320]{3,2,1,0:T(8,128)} %fusion.195, f32[3,32,32,320]{3,2,1,0:T(8,128)} %fusion.194, f32[3,32,32,320]{3,2,1,0:T(8,128)} %fusion.193, f32[3,32,32,320]{3,2,1,0:T(8,128)} %fusion.192, ...), kind=kOutput, calls=%fused_computation.51 | convolution fusion | flops 320471040 | bytes 29220864 | tf_op jit(solution)/shard_map/bhwo,co->bhwc/dot_general | solution.py:224
  528.1 4.7 multiply_convert_fusion.1
  536.3 3.7 fusion.169
  540.1 3.8 fusion.167
  543.9 3.8 fusion.166
  555.1 3.7 fusion.163
  565.2 4.7 copy.135
  570.0 4.4 reshape.186
  574.5 3.9 fusion.147
  580.6 10.7 pad_add_fusion.2
  606.4 6.7 copy.131
  613.0 6.0 reshape.182
  635.2 4.8 concatenate.92
  652.7 4.4 concatenate.91
  657.1 4.3 pad_maximum_fusion
  661.4 9.8 copy.133
  671.2 8.1 reshape.184
  692.3 3.9 fusion.124
  706.4 7.6 copy.43
  716.4 5.7 convolution_bitcast_fusion.4
  724.2 212.3 %all-reduce.56 = (bf16[2,320,160]{2,0,1:T(2,128)(2,1)S(1)}, bf16[2,1280,320]{2,0,1:T(2,128)(2,1)}) all-reduce(f32[2,320,160]{2,0,1:T(2,128)S(1)} %copy.41, f32[2,1280,320]{2,0,1:T(2,128)} %copy.43), channel_id=5, replica_groups=mesh['dp'=8,'grp'=4] {'dp'}, use_global_device_ids=true, to_apply=%region_14.15.clone | all-reduce | flops 921600 | bytes 5529600
  951.0 11.1 %pad_add_fusion = f32[3,33,33,320]{3,2,1,0:T(8,128)} fusion(f32[3,32,32,320]{3,2,1,0:T(8,128)} %fusion.202, f32[3,32,32,320]{3,2,1,0:T(8,128)} %fusion.201, f32[3,32,32,320]{3,2,1,0:T(8,128)} %fusion.200, f32[3,32,32,320]{3,2,1,0:T(8,128)} %fusion.199), kind=kLoop, calls=%fused_computation.20 | loop fusion | flops 3136320 | bytes 19910400 | tf_op jit(solution)/shard_map/add | solution.py:61
  978.9 10.2 pad_add_fusion.1
  989.2 3.7 fusion.30
  992.9 3.8 fusion.26
  1003.6 39.0 %psum.55 = f32[2,1120]{1,0:T(2,128)} all-reduce(f32[2,1120]{1,0:T(2,128)S(1)} %pad_maximum_fusion.9), channel_id=1, replica_groups=mesh['dp'=8,'grp'=4] {'dp','grp'}, use_global_device_ids=true, to_apply=%region_29.30 | all-reduce | flops 2240 | bytes 17920 | tf_op jit(solution)/shard_map/psum | solution.py:278
  1042.7 11.6 %psum.52 = bf16[2,40,160]{2,0,1:T(2,128)(2,1)S(1)} all-reduce(bf16[2,40,160]{2,0,1:T(2,128)(2,1)S(1)} %dynamic-slice_convert_fusion.1), channel_id=1, replica_groups=mesh['dp'=8,'grp'=4] {'grp'}, use_global_device_ids=true, to_apply=%region_15.16 | all-reduce | flops 12800 | bytes 51200 | tf_op jit(solution)/shard_map/psum | solution.py:272
  1059.7 20.5 %psum.54 = f32[2,1120]{1,0:T(2,128)S(1)} all-reduce(f32[2,1120]{1,0:T(2,128)S(1)} %concatenate.97), channel_id=1, replica_groups=mesh['dp'=8,'grp'=4] {'dp'}, use_global_device_ids=true, to_apply=%region_20.21 | all-reduce | flops 2240 | bytes 17920 | tf_op jit(solution)/shard_map/psum | solution.py:282
  (472 shorter events, 343.6 us)
Async XLA Ops:
  7.2 98.6 %all-gather.4.cloned.1.call-start = ((), (), s32[]{:S(2)}) async-start(), calls=%async_computation.3 | async-start | bytes 2211840 | tf_op jit(solution)/shard_map/all_gather | solution.py:137
  9.1 129.5 %all-gather.8.cloned.1.call-start = ((), (), s32[]{:S(2)}) async-start(), calls=%async_computation.5 | async-start | bytes 2211840 | tf_op jit(solution)/shard_map/all_gather | solution.py:141
  9.9 170.8 %all-gather.6.cloned.1.call-start = ((), (), s32[]{:S(2)}) async-start(), calls=%async_computation.4 | async-start | bytes 3317760 | tf_op jit(solution)/shard_map/all_gather | solution.py:138
  11.8 985.0 %reduce-scatter.14.cloned.1.call-start = ((), (), s32[]{:S(2)}) async-start(), calls=%async_computation.8 | async-start | bytes 2211840
  102.3 18.7 %copy-start.16 = (bf16[3,32,32,320]{3,2,1,0:T(8,128)(2,1)}, bf16[3,32,32,320]{3,2,1,0:T(8,128)(2,1)S(1)}, u32[]{:S(2)}) copy-start(bf16[3,32,32,320]{3,2,1,0:T(8,128)(2,1)S(1)} %fusion.3) | copy-start | bytes 5898244
  114.1 12.1 %copy-start.110 = (f32[2,160]{1,0:T(2,128)}, f32[2,160]{1,0:T(2,128)S(1)}, u32[]{:S(2)}) copy-start(f32[2,160]{1,0:T(2,128)S(1)} %get-tuple-element.100) | copy-start | bytes 3844
  124.6 76.7 %copy-start.18 = (bf16[3,32,32,320]{3,2,1,0:T(8,128)(2,1)}, bf16[3,32,32,320]{3,2,1,0:T(8,128)(2,1)S(1)}, u32[]{:S(2)}) copy-start(bf16[3,32,32,320]{3,2,1,0:T(8,128)(2,1)S(1)} %fusion.5) | copy-start | bytes 5898244
  127.4 250.1 %copy-start.69 = (bf16[2,1280,160]{1,2,0:T(8,128)(2,1)}, bf16[2,1280,160]{1,2,0:T(8,128)(2,1)S(1)}, u32[]{:S(2)}) copy-start(bf16[2,1280,160]{1,2,0:T(8,128)(2,1)S(1)} %fusion.120) | copy-start | bytes 2457604
  183.9 76.4 %copy-start.102 = (f32[2,320]{1,0:T(2,128)}, f32[2,320]{1,0:T(2,128)S(1)}, u32[]{:S(2)}) copy-start(f32[2,320]{1,0:T(2,128)S(1)} %get-tuple-element.97) | copy-start | bytes 7684
  184.5 103.5 %copy-start.47 = (bf16[2,1920,320]{2,1,0:T(8,128)(2,1)}, bf16[2,1920,320]{2,1,0:T(8,128)(2,1)S(1)}, u32[]{:S(2)}) copy-start(bf16[2,1920,320]{2,1,0:T(8,128)(2,1)S(1)} %fusion.1) | copy-start | bytes 7372804
  211.4 85.7 %copy-start.33 = (f32[3,32,32,160]{3,2,1,0:T(8,128)}, f32[3,32,32,160]{3,2,1,0:T(8,128)S(1)}, u32[]{:S(2)}) copy-start(f32[3,32,32,160]{3,2,1,0:T(8,128)S(1)} %get-tuple-element.78) | copy-start | bytes 5898244
  213.6 38.4 %copy-start.5 = (bf16[3,32,32,320]{3,2,1,0:T(8,128)(2,1)}, bf16[3,32,32,320]{3,2,1,0:T(8,128)(2,1)S(1)}, u32[]{:S(2)}) copy-start(bf16[3,32,32,320]{3,2,1,0:T(8,128)(2,1)S(1)} %fusion.7) | copy-start | bytes 5898244
  233.2 54.8 %copy-start.20 = (bf16[3,32,32,320]{3,2,1,0:T(8,128)(2,1)}, bf16[3,32,32,320]{3,2,1,0:T(8,128)(2,1)S(1)}, u32[]{:S(2)}) copy-start(bf16[3,32,32,320]{3,2,1,0:T(8,128)(2,1)S(1)} %fusion.9) | copy-start | bytes 5898244
  274.7 48.0 %copy-start.39 = (f32[3,32,32,160]{3,2,1,0:T(8,128)}, f32[3,32,32,160]{3,2,1,0:T(8,128)S(1)}, u32[]{:S(2)}) copy-start(f32[3,32,32,160]{3,2,1,0:T(8,128)S(1)} %get-tuple-element.76) | copy-start | bytes 5898244
  300.4 11.2 %copy-start.46 = (f32[3,32,32,160]{3,2,1,0:T(8,128)}, f32[3,32,32,160]{3,2,1,0:T(8,128)S(1)}, u32[]{:S(2)}) copy-start(f32[3,32,32,160]{3,2,1,0:T(8,128)S(1)} %get-tuple-element.74) | copy-start | bytes 5898244
  329.1 11.3 %copy-start.8 = (bf16[3,32,32,320]{3,2,1,0:T(8,128)(2,1)}, bf16[3,32,32,320]{3,2,1,0:T(8,128)(2,1)S(1)}, u32[]{:S(2)}) copy-start(bf16[3,32,32,320]{3,2,1,0:T(8,128)(2,1)S(1)} %get-tuple-element.60) | copy-start | bytes 5898244
  361.6 19.0 %copy-start.12 = (bf16[3,32,32,160]{3,2,1,0:T(8,128)(2,1)}, bf16[3,32,32,160]{3,2,1,0:T(8,128)(2,1)S(1)}, u32[]{:S(2)}) copy-start(bf16[3,32,32,160]{3,2,1,0:T(8,128)(2,1)S(1)} %get-tuple-element.62) | copy-start | bytes 2949124
  383.7 11.1 %copy-start.75 = (bf16[3,32,32,160]{3,2,1,0:T(8,128)(2,1)S(1)}, bf16[3,32,32,160]{3,2,1,0:T(8,128)(2,1)}, u32[]{:S(2)}) copy-start(bf16[3,32,32,160]{3,2,1,0:T(8,128)(2,1)} %param.16) | copy-start | bytes 2949124
  383.7 25.7 %slice-start.2 = ((s8[4718592]{0:T(1024)(128)(4,1)}), s8[524288]{0:T(1024)(128)(4,1)S(1)}, s32[]{:S(2)}) async-start(s8[4718592]{0:T(1024)(128)(4,1)} %bitcast.644), calls=%async_computation.12 | async-start | bytes 1048576
  394.8 14.6 %slice-start.3 = ((s8[4718592]{0:T(1024)(128)(4,1)}), s8[4194304]{0:T(1024)(128)(4,1)S(1)}, s32[]{:S(2)}) async-start(s8[4718592]{0:T(1024)(128)(4,1)} %bitcast.644), calls=%async_computation.13 | async-start | bytes 8388608
  418.4 11.2 %copy-start.10 = (bf16[3,32,32,320]{3,2,1,0:T(8,128)(2,1)}, bf16[3,32,32,320]{3,2,1,0:T(8,128)(2,1)S(1)}, u32[]{:S(2)}) copy-start(bf16[3,32,32,320]{3,2,1,0:T(8,128)(2,1)S(1)} %get-tuple-element.115) | copy-start | bytes 5898244
  433.4 11.0 %copy-start.90 = (u32[3,32,160]{2,1,0:T(8,128)S(1)}, u32[3,32,160]{2,1,0:T(8,128)}, u32[]{:S(2)}) copy-start(u32[3,32,160]{2,1,0:T(8,128)} %get-tuple-element.35) | copy-start | bytes 184324
  433.4 11.0 %copy-start.91 = (u32[3,32,160]{2,1,0:T(8,128)S(1)}, u32[3,32,160]{2,1,0:T(8,128)}, u32[]{:S(2)}) copy-start(u32[3,32,160]{2,1,0:T(8,128)} %get-tuple-element.36) | copy-start | bytes 184324
  451.0 63.3 %copy-start.14 = (bf16[3,32,32,160]{3,2,1,0:T(8,128)(2,1)}, bf16[3,32,32,160]{3,2,1,0:T(8,128)(2,1)S(1)}, u32[]{:S(2)}) copy-start(bf16[3,32,32,160]{3,2,1,0:T(8,128)(2,1)S(1)} %get-tuple-element.54) | copy-start | bytes 2949124
  475.7 8.8 copy-start.88
  475.7 8.8 copy-start.89
  487.5 23.7 %copy-start.4 = (bf16[3,32,32,160]{3,2,1,0:T(8,128)(2,1)}, bf16[3,32,32,160]{3,2,1,0:T(8,128)(2,1)S(1)}, u32[]{:S(2)}) copy-start(bf16[3,32,32,160]{3,2,1,0:T(8,128)(2,1)S(1)} %get-tuple-element.66) | copy-start | bytes 2949124
  511.2 15.9 %slice-start = ((s8[4718592]{0:T(1024)(128)(4,1)}), s8[524288]{0:T(1024)(128)(4,1)S(1)}, s32[]{:S(2)}) async-start(s8[4718592]{0:T(1024)(128)(4,1)} %bitcast.642), calls=%async_computation.10 | async-start | bytes 1048576
  514.3 12.8 %slice-start.1 = ((s8[4718592]{0:T(1024)(128)(4,1)}), s8[4194304]{0:T(1024)(128)(4,1)S(1)}, s32[]{:S(2)}) async-start(s8[4718592]{0:T(1024)(128)(4,1)} %bitcast.642), calls=%async_computation.11 | async-start | bytes 8388608
  514.3 12.8 %copy-start.34 = (f32[3,32,32,160]{3,2,1,0:T(8,128)S(1)}, f32[3,32,32,160]{3,2,1,0:T(8,128)}, u32[]{:S(2)}) copy-start(f32[3,32,32,160]{3,2,1,0:T(8,128)} %copy-done.33) | copy-start | bytes 5898244
  514.3 13.8 %copy-start.45 = (f32[3,32,32,160]{3,2,1,0:T(8,128)S(1)}, f32[3,32,32,160]{3,2,1,0:T(8,128)}, u32[]{:S(2)}) copy-start(f32[3,32,32,160]{3,2,1,0:T(8,128)} %copy-done.44) | copy-start | bytes 5898244
  535.7 19.4 %copy-start = (bf16[3,32,32,320]{3,2,1,0:T(8,128)(2,1)}, bf16[3,32,32,320]{3,2,1,0:T(8,128)(2,1)S(1)}, u32[]{:S(2)}) copy-start(bf16[3,32,32,320]{3,2,1,0:T(8,128)(2,1)S(1)} %get-tuple-element.56) | copy-start | bytes 5898244
  574.4 424.4 %reduce-scatter.10.cloned.1.call-start = ((), (), s32[]{:S(2)}) async-start(), calls=%async_computation.6 | async-start | bytes 3317760
  580.6 10.7 copy-start.32
  580.6 10.7 copy-start.86
  580.6 10.7 copy-start.87
  619.0 381.8 %reduce-scatter.12.cloned.1.call-start = ((), (), s32[]{:S(2)}) async-start(), calls=%async_computation.7 | async-start | bytes 5529600
  682.3 372.2 %all-reduce.55.cloned.1.call-start = ((), (), s32[]{:S(2)}) async-start(), calls=%async_computation.9 | async-start | bytes 1802240 | tf_op jit(solution)/shard_map/psum | solution.py:269
  722.1 216.2 %copy-start.15 = (bf16[3,32,32,160]{3,2,1,0:T(8,128)(2,1)S(1)}, bf16[3,32,32,160]{3,2,1,0:T(8,128)(2,1)}, u32[]{:S(2)}) copy-start(bf16[3,32,32,160]{3,2,1,0:T(8,128)(2,1)} %copy-done.14) | copy-start | bytes 2949124
  722.1 216.2 %copy-start.70 = (bf16[2,1280,160]{1,2,0:T(8,128)(2,1)S(1)}, bf16[2,1280,160]{1,2,0:T(8,128)(2,1)}, u32[]{:S(2)}) copy-start(bf16[2,1280,160]{1,2,0:T(8,128)(2,1)} %copy-done.69) | copy-start | bytes 2457604
  951.0 11.1 %copy-start.3 = (bf16[3,32,32,160]{3,2,1,0:T(8,128)(2,1)S(1)}, bf16[3,32,32,160]{3,2,1,0:T(8,128)(2,1)}, u32[]{:S(2)}) copy-start(bf16[3,32,32,160]{3,2,1,0:T(8,128)(2,1)} %copy-done.2) | copy-start | bytes 2949124
  951.0 11.1 %copy-start.63 = (bf16[2,1920,160]{1,2,0:T(8,128)(2,1)S(1)}, bf16[2,1920,160]{1,2,0:T(8,128)(2,1)}, u32[]{:S(2)}) copy-start(bf16[2,1920,160]{1,2,0:T(8,128)(2,1)} %copy-done.60) | copy-start | bytes 3686404
  975.8 13.3 %slice-start.6 = ((s8[6082560]{0:T(1024)(128)(4,1)}), s8[4194304]{0:T(1024)(128)(4,1)S(1)}, s32[]{:S(2)}) async-start(s8[6082560]{0:T(1024)(128)(4,1)} %bitcast.648), calls=%async_computation.16 | async-start | bytes 8388608
  978.9 10.2 copy-start.43
  978.9 10.2 slice-start.7
  978.9 10.2 copy-start.52
  996.7 57.6 %copy-start.93 = (bf16[2,40,160]{2,1,0:T(8,128)(2,1)S(1)}, bf16[2,40,160]{2,1,0:T(8,128)(2,1)}, u32[]{:S(2)}) copy-start(bf16[2,40,160]{2,1,0:T(8,128)(2,1)} %param.20) | copy-start | bytes 76804
  996.7 57.6 %copy-start.112 = (f32[2,160]{1,0:T(2,128)S(1)}, f32[2,160]{1,0:T(2,128)}, u32[]{:S(2)}) copy-start(f32[2,160]{1,0:T(2,128)} %get-tuple-element.106) | copy-start | bytes 3844
  996.7 57.7 %copy-start.78 = (bf16[2,240,160]{1,2,0:T(8,128)(2,1)S(1)}, bf16[2,240,160]{1,2,0:T(8,128)(2,1)}, u32[]{:S(2)}) copy-start(bf16[2,240,160]{1,2,0:T(8,128)(2,1)} %param.17) | copy-start | bytes 460804
  996.7 57.7 %copy-start.113 = (f32[2,160]{1,0:T(2,128)S(1)}, f32[2,160]{1,0:T(2,128)}, u32[]{:S(2)}) copy-start(f32[2,160]{1,0:T(2,128)} %get-tuple-element.104) | copy-start | bytes 3844
  996.7 59.0 %copy-start.76 = (bf16[2,240,320]{1,2,0:T(8,128)(2,1)S(1)}, bf16[2,240,320]{1,2,0:T(8,128)(2,1)}, u32[]{:S(2)}) copy-start(bf16[2,240,320]{1,2,0:T(8,128)(2,1)} %param.18) | copy-start | bytes 921604
  996.7 59.0 %copy-start.107 = (f32[2,320]{1,0:T(2,128)S(1)}, f32[2,320]{1,0:T(2,128)}, u32[]{:S(2)}) copy-start(f32[2,320]{1,0:T(2,128)} %get-tuple-element.102) | copy-start | bytes 7684
  996.7 60.3 %copy-start.77 = (bf16[2,160,320]{2,1,0:T(8,128)(2,1)S(1)}, bf16[2,160,320]{2,1,0:T(8,128)(2,1)}, u32[]{:S(2)}) copy-start(bf16[2,160,320]{2,1,0:T(8,128)(2,1)} %param.21) | copy-start | bytes 614404
  996.8 60.3 %copy-start.104 = (f32[2,320]{1,0:T(2,128)S(1)}, f32[2,320]{1,0:T(2,128)}, u32[]{:S(2)}) copy-start(f32[2,320]{1,0:T(2,128)} %get-tuple-element.103) | copy-start | bytes 7684
  996.8 61.7 %copy-start.79 = (bf16[2,160,160]{1,2,0:T(8,128)(2,1)S(1)}, bf16[2,160,160]{1,2,0:T(8,128)(2,1)}, u32[]{:S(2)}) copy-start(bf16[2,160,160]{1,2,0:T(8,128)(2,1)} %copy.39) | copy-start | bytes 307204
  996.8 61.6 %copy-start.114 = (f32[2,160]{1,0:T(2,128)S(1)}, f32[2,160]{1,0:T(2,128)}, u32[]{:S(2)}) copy-start(f32[2,160]{1,0:T(2,128)} %get-tuple-element.105) | copy-start | bytes 3844
  998.0 82.4 %copy-start.111 = (f32[2,160]{1,0:T(2,128)S(1)}, f32[2,160]{1,0:T(2,128)}, u32[]{:S(2)}) copy-start(f32[2,160]{1,0:T(2,128)} %copy-done.110) | copy-start | bytes 3844
  1000.8 81.6 %copy-start.109 = (f32[2,160]{1,0:T(2,128)S(1)}, f32[2,160]{1,0:T(2,128)}, u32[]{:S(2)}) copy-start(f32[2,160]{1,0:T(2,128)} %copy-done.108) | copy-start | bytes 3844
  1000.8 82.3 %copy-start.116 = (f32[2,160]{1,0:T(2,128)S(1)}, f32[2,160]{1,0:T(2,128)}, u32[]{:S(2)}) copy-start(f32[2,160]{1,0:T(2,128)} %copy-done.115) | copy-start | bytes 3844
  1002.2 81.8 %copy-start.103 = (f32[2,320]{1,0:T(2,128)S(1)}, f32[2,320]{1,0:T(2,128)}, u32[]{:S(2)}) copy-start(f32[2,320]{1,0:T(2,128)} %copy-done.102) | copy-start | bytes 7684
  1054.4 28.7 %copy-start.84 = (bf16[2,240,160]{1,2,0:T(8,128)(2,1)S(1)}, bf16[2,240,160]{1,2,0:T(8,128)(2,1)}, u32[]{:S(2)}) copy-start(bf16[2,240,160]{1,2,0:T(8,128)(2,1)} %get-tuple-element.47) | copy-start | bytes 460804
  1054.4 29.6 %copy-start.81 = (bf16[2,160,320]{2,0,1:T(2,128)(2,1)S(1)}, bf16[2,160,320]{2,0,1:T(2,128)(2,1)}, u32[]{:S(2)}) copy-start(bf16[2,160,320]{2,0,1:T(2,128)(2,1)} %get-tuple-element.50) | copy-start | bytes 614404
  1054.5 30.8 %copy-start.80 = (bf16[2,240,320]{1,2,0:T(8,128)(2,1)S(1)}, bf16[2,240,320]{1,2,0:T(8,128)(2,1)}, u32[]{:S(2)}) copy-start(bf16[2,240,320]{1,2,0:T(8,128)(2,1)} %get-tuple-element.48) | copy-start | bytes 921604
  1054.5 30.8 %copy-start.106 = (f32[2,320]{1,0:T(2,128)S(1)}, f32[2,320]{1,0:T(2,128)}, u32[]{:S(2)}) copy-start(f32[2,320]{1,0:T(2,128)} %copy-done.105) | copy-start | bytes 7684
  (75 other events, 285.6 us)
Sparse Core Ops, SparseCore 0:
  10.8 57.5 all-gather.3
  70.6 49.5 all-gather.7
  123.0 57.5 all-gather.5
  574.5 65.3 reduce-scatter.13
  643.7 71.8 reduce-scatter.9
  719.1 166.6 reduce-scatter.11
  1003.7 34.4 all-reduce.54
where the time goes:
time: 1100 us; the launch traced here: 1090 us
  matrix products  364 us (33%)
  blocking collectives  354 us (32%)
  other arithmetic  207 us (19%)
  local copies, waits for them, and re-layouts  110 us (10%)
  waiting for transfers between devices  40.8 us (4%)
  between operations  17.5 us (2%)
    unnamed x1, blocking collectives  212 us
    dot_general x40, matrix products, conv_input_grad(): jnp.einsum('bhwo,co->bhwc', grad_out, weight_tap, preferred_element_type=...  132 us
    dot_general x40, matrix products, conv_apply(): jnp.einsum('bhwc,co->bhwo', window, weight_tap, preferred_element_type=jn...  116 us
    dot_general x40, matrix products, conv_weight_grad(): jnp.einsum('bhwc,bhwo->co', window, grad_out, preferred_element_type=jnp....  76.2 us
    add x7, other arithmetic, conv_input_grad(): summed = placed if summed is None else summed + placed  73.9 us
    unnamed x285, local copies, waits for them, and re-layouts  65.9 us
    all_gather x1, waiting for transfers between devices, on_device(): lax.all_gather(v_down2, 'dp', axis=1, tiled=True)  40 us
    psum x1, blocking collectives, on_device(): bias_sum = lax.psum(bias_local, ('dp', 'grp'))  39 us
  transfers between devices with their start and end apart: 7, of which 1 were waited for; matrix products, arithmetic and copies ran while one was open for 25% of the time, Pallas kernels for 0%

commit v1 on v0

v1 whole, which is shorter than its diff:
```python
import functools
import jax
import jax.numpy as jnp
from jax import lax
from jax.experimental import pallas as pl
from jax.experimental.pallas import tpu as pltpu
from jax.sharding import PartitionSpec as P

BF = jnp.bfloat16
F32 = jnp.float32
LAYERS = 2
C = 160
C2 = 320
SPANS = ((0, 160), (160, 480), (480, 640), (640, 800), (800, 1120))


def nt(a, b):
    return lax.dot_general(a, b, (((1,), (1,)), ((), ())), preferred_element_type=F32)


def nn(a, b):
    return lax.dot_general(a, b, (((1,), (0,)), ((), ())), preferred_element_type=F32)


def eye(n):
    same = lax.broadcasted_iota(jnp.int32, (n, n), 0) == lax.broadcasted_iota(jnp.int32, (n, n), 1)
    return jnp.where(same, 1.0, 0.0).astype(BF)


def lane():
    return lax.broadcasted_iota(jnp.int32, (1, 128), 1)


def keep(cond, tile):
    return jnp.where(cond, tile, jnp.zeros((), tile.dtype))


def col_shift(tile, off):
    if off == 0:
        return tile
    col = lane() & 31
    if off == 1:
        return keep(col != 31, pltpu.roll(tile, 127, 1))
    return keep(col != 0, pltpu.roll(tile, 1, 1))


def row_before(tile):
    return keep(lane() >= 32, pltpu.roll(tile, 32, 1))


def row_after(tile):
    return keep(lane() < 96, pltpu.roll(tile, 96, 1))


def at(v):
    return slice(v * 128, (v + 1) * 128)


def put_down(ext, v, tile):
    n = tile.shape[0]
    for c in range(3):
        moved = col_shift(tile, c - 1)
        ext[c * n : (c + 1) * n, at(v + 1)] = moved
        if v == 7:
            ext[c * n : (c + 1) * n, at(0)] = row_before(moved)


def put_right(ext, v, tile):
    n = tile.shape[0]
    for c in range(2):
        moved = col_shift(tile, c - 1)
        ext[(2 + c) * n : (3 + c) * n, at(v)] = moved
        if v == 7:
            ext[c * n : (c + 1) * n, at(0)] = row_before(moved)
        else:
            ext[c * n : (c + 1) * n, at(v + 1)] = moved


def put_down_back(ext, v, tile):
    n = tile.shape[0]
    for c in range(3):
        moved = col_shift(tile, 1 - c)
        ext[c * n : (c + 1) * n, at(v)] = moved
        if v == 0:
            ext[c * n : (c + 1) * n, at(8)] = row_after(moved)


def put_right_back(ext, v, tile):
    n = tile.shape[0]
    for c in range(2):
        moved = col_shift(tile, 1 - c)
        ext[(2 + c) * n : (3 + c) * n, at(v)] = moved
        if v == 0:
            ext[c * n : (c + 1) * n, at(7)] = row_after(moved)
        else:
            ext[c * n : (c + 1) * n, at(v - 1)] = moved


def pair_elu(x):
    e = jnp.exp(-jnp.abs(x)) - 1.0
    up = x > 0
    return jnp.concatenate([jnp.where(up, x, e), jnp.where(up, e, -x)], axis=0).astype(BF)


def elu_back(grad, act):
    slope = jnp.minimum(act.astype(F32), 0.0) + 1.0
    both = grad * slope
    return both[:C] - both[C:]


def sigmoid(x):
    return 1.0 / (1.0 + jnp.exp(-x))


def load_cells(ref, v):
    rows = jnp.concatenate([ref[g * 8 + v] for g in range(4)], axis=0)
    return nt(eye(C), rows)


def store_bf16(ref, v, tile):
    out = nt(eye(128), tile.astype(BF)).astype(BF)
    for g in range(4):
        ref[g * 8 + v] = out[g * 32 : (g + 1) * 32]


def store_f32(ref, v, tile):
    out = tile.T
    for g in range(4):
        ref[g * 8 + v] = out[g * 32 : (g + 1) * 32]


def scale_of(total, gain):
    return gain * lax.rsqrt(total)


def transpose_weight(v_ref, first, rows, width, dest):
    unit = eye(width)
    part = 320
    for k in range(rows // part):
        block = v_ref[first + k * part : first + (k + 1) * part, :]
        dest[:, k * part : (k + 1) * part] = nt(unit, block).astype(BF)


def square_sum(ref):
    vals = ref[...].astype(F32)
    return jnp.sum(vals * vals, axis=1, keepdims=True)


def fwd_kernel(
    down_in, right_in, v1, v2, r1, vs, r2, cols,
    down_out, right_out, cells, actd, actr, acth, gated, gater, kappa,
    w1, w2, wr1, ws, wr2, ext, ext4, dflow, rflow,
):
    @pl.when(pl.program_id(0) == 0)
    def _():
        for l in range(LAYERS):
            for a in range(2):
                transpose_weight(v1.at[l], a * 960, 960, 160, w1.at[l, a])
                transpose_weight(v2.at[l], a * 960, 960, 320, w2.at[l, a])
            transpose_weight(r1.at[l], 0, 1280, 160, wr1.at[l])
            transpose_weight(vs.at[l], 0, 320, 160, ws.at[l])
            transpose_weight(r2.at[l], 0, 1280, 320, wr2.at[l])
            totals = (
                square_sum(w1.at[l, 0]) + square_sum(w1.at[l, 1]),
                square_sum(w2.at[l, 0]) + square_sum(w2.at[l, 1]),
                square_sum(wr1.at[l]),
                square_sum(ws.at[l]),
                square_sum(wr2.at[l]),
            )
            for total, (lo, hi) in zip(totals, SPANS):
                kappa[lo:hi, l : l + 1] = scale_of(total, cols[lo:hi, l : l + 1])

    for v in range(8):
        x = load_cells(down_in.at[0], v)
        dflow[:, at(v)] = x
        act = pair_elu(x)
        cells[0, 0, :, at(v)] = act
        put_down(ext, v, act)
        rflow[:, at(v)] = load_cells(right_in.at[0], v)
    for l in range(LAYERS):
        def scale(m):
            lo, hi = SPANS[m]
            return kappa[lo:hi, l : l + 1]

        def bias(m):
            lo, hi = SPANS[m]
            return cols[lo:hi, 2 + l : 3 + l]

        for j in range(4):
            acc = nn(w1[l, 0], ext[:, j * 256 : j * 256 + 256])
            acc = acc + nn(w1[l, 1], ext[:, j * 256 + 128 : j * 256 + 384])
            for h in range(2):
                v = 2 * j + h
                actd[0, l, :, at(v)] = pair_elu(acc[:, at(h)] * scale(0) + bias(0))
        for v in range(8):
            put_down(ext, v, actd[0, l, :, at(v)])
            act = pair_elu(rflow[:, at(v)])
            actr[0, l, :, at(v)] = act
            put_right(ext4, v, act)
        for j in range(4):
            acc = nn(w2[l, 0], ext[:, j * 256 : j * 256 + 256])
            acc = acc + nn(w2[l, 1], ext[:, j * 256 + 128 : j * 256 + 384])
            for h in range(2):
                v = 2 * j + h
                gate = acc[:, at(h)] * scale(1) + bias(1)
                t = gate[:C]
                s = sigmoid(gate[C:])
                gated[0, l, :C, at(v)] = t.astype(BF)
                gated[0, l, C:, at(v)] = s.astype(BF)
                new = dflow[:, at(v)] + t * s
                dflow[:, at(v)] = new
                cells[0, l + 1, :, at(v)] = pair_elu(new)
        skip_bias = bias(2) + bias(3)
        for j in range(4):
            acc = nn(wr1[l], ext4[:, j * 256 : j * 256 + 256]) * scale(2)
            acc = acc + nn(ws[l], cells[0, l + 1, :, j * 256 : j * 256 + 256]) * scale(3)
            for h in range(2):
                v = 2 * j + h
                acth[0, l, :, at(v)] = pair_elu(acc[:, at(h)] + skip_bias)
        for v in range(8):
            put_right(ext4, v, acth[0, l, :, at(v)])
            if l + 1 < LAYERS:
                put_down(ext, v, cells[0, l + 1, :, at(v)])
        for j in range(4):
            acc = nn(wr2[l], ext4[:, j * 256 : j * 256 + 256])
            for h in range(2):
                v = 2 * j + h
                gate = acc[:, at(h)] * scale(4) + bias(4)
                t = gate[:C]
                s = sigmoid(gate[C:])
                gater[0, l, :C, at(v)] = t.astype(BF)
                gater[0, l, C:, at(v)] = s.astype(BF)
                rflow[:, at(v)] = rflow[:, at(v)] + t * s
    for v in range(8):
        store_bf16(down_out.at[0], v, dflow[:, at(v)])
        store_bf16(right_out.at[0], v, rflow[:, at(v)])


def taps_beside(v_ref, first, count, dest):
    n = v_ref.shape[1]
    for k in range(count):
        dest[:, k * n : (k + 1) * n] = v_ref[first + k * C2 : first + (k + 1) * C2, :]


def gate_back(g, t, s):
    p = g * s
    q = p * t * (1.0 - s)
    return jnp.concatenate([p, q], axis=0)


def bwd_kernel(
    top, down_g, right_g, mask, *refs,
):
    refs = list(refs)
    cells_g = None if top else refs.pop(0)
    (
        low_cells, high_cells, actd, actr, acth, gated, gater, kappa, v1, v2, r1, vs, r2,
    ) = refs[:13]
    refs = refs[13:]
    if top:
        down_out, right_out, cells_out = refs[:3]
        refs = refs[3:]
    else:
        down_out, right_out = refs[:2]
        refs = refs[2:]
    (
        o1, o2, or1, os, or2, obias,
        b1, b2, br1, br2, g1, g2, gr1, gs, gr2, bsum, ext, ext1, ext4, ext41, dskip, gdown, gright,
    ) = refs
    layer = 1 if top else 0
    step = pl.program_id(0)

    @pl.when(step == 0)
    def _():
        for a in range(2):
            taps_beside(v1.at[0], a * 960, 3, b1.at[a])
            taps_beside(v2.at[0], a * 960, 3, b2.at[a])
        taps_beside(r1.at[0], 0, 4, br1)
        taps_beside(r2.at[0], 0, 4, br2)
        for acc in (g1, g2, gr1, gs, gr2, bsum):
            acc[...] = jnp.zeros(acc.shape, F32)

    def scale(m):
        lo, hi = SPANS[m]
        return kappa[lo:hi, layer : layer + 1]

    def add_bias(m, total):
        lo, hi = SPANS[m]
        bsum[lo:hi, :] += total

    total = None
    for v in range(8):
        if top:
            m = mask[0, :, at(v)]
            gdown[:, at(v)] = load_cells(down_g.at[0], v) * m
            g = load_cells(right_g.at[0], v) * m
            gright[:, at(v)] = g
        else:
            g = right_g[0, :, at(v)]
        d = gate_back(g, gater[0, 0, :C, at(v)].astype(F32), gater[0, 0, C:, at(v)].astype(F32))
        total = d if total is None else total + d
        put_right_back(ext4, v, (d * scale(4)).astype(BF))
    add_bias(4, total)
    gr2[...] += nt(acth[0, 0], ext4[...])
    total = None
    for j in range(4):
        e = nn(br2[...], ext4[:, j * 256 : j * 256 + 256])
        for h in range(2):
            v = 2 * j + h
            d = elu_back(e[:, at(h)], acth[0, 0, :, at(v)])
            total = d if total is None else total + d
            put_right_back(ext41, v, (d * scale(2)).astype(BF))
            dskip[:, at(v)] = (d * scale(3)).astype(BF)
    add_bias(2, total)
    add_bias(3, total)
    gr1[...] += nt(actr[0, 0], ext41[...])
    gs[...] += nt(high_cells[0, 0], dskip[...])
    for j in range(4):
        e = nn(br1[...], ext41[:, j * 256 : j * 256 + 256])
        k = nn(vs[0], dskip[:, j * 256 : j * 256 + 256])
        for h in range(2):
            v = 2 * j + h
            old = gright[:, at(v)] if top else right_g[0, :, at(v)]
            new = old + elu_back(e[:, at(h)], actr[0, 0, :, at(v)])
            if top:
                right_out[0, :, at(v)] = new
            else:
                store_f32(right_out.at[0], v, new)
            gc = k[:, at(h)]
            if not top:
                gc = gc + cells_g[0, :, at(v)]
            old = gdown[:, at(v)] if top else down_g[0, :, at(v)]
            gdown[:, at(v)] = old + elu_back(gc, high_cells[0, 0, :, at(v)])
    total = None
    for v in range(8):
        g = gdown[:, at(v)]
        if top:
            down_out[0, :, at(v)] = g
        d = gate_back(g, gated[0, 0, :C, at(v)].astype(F32), gated[0, 0, C:, at(v)].astype(F32))
        total = d if total is None else total + d
        put_down_back(ext, v, (d * scale(1)).astype(BF))
    add_bias(1, total)
    for a in range(2):
        lo = 128 * (1 - a)
        g2[a] += nt(actd[0, 0], ext[:, lo : lo + 1024])
    total = None
    for j in range(4):
        e = nn(b2[1], ext[:, j * 256 : j * 256 + 256])
        e = e + nn(b2[0], ext[:, j * 256 + 128 : j * 256 + 384])
        for h in range(2):
            v = 2 * j + h
            d = elu_back(e[:, at(h)], actd[0, 0, :, at(v)])
            total = d if total is None else total + d
            put_down_back(ext1, v, (d * scale(0)).astype(BF))
    add_bias(0, total)
    for a in range(2):
        lo = 128 * (1 - a)
        g1[a] += nt(low_cells[0, 0], ext1[:, lo : lo + 1024])
    for j in range(4):
        e = nn(b1[1], ext1[:, j * 256 : j * 256 + 256])
        e = e + nn(b1[0], ext1[:, j * 256 + 128 : j * 256 + 384])
        if top:
            cells_out[0, :, j * 256 : j * 256 + 256] = e
        else:
            for h in range(2):
                v = 2 * j + h
                last = gdown[:, at(v)] + elu_back(e[:, at(h)], low_cells[0, 0, :, at(v)])
                store_f32(down_out.at[0], v, last)

    @pl.when(step == pl.num_programs(0) - 1)
    def _():
        for a in range(2):
            for c in range(3):
                row = (a * 3 + c) * C2
                o1[row : row + C2, :] = g1[a, :, c * C : (c + 1) * C].astype(BF)
                o2[row : row + C2, :] = g2[a, :, c * C2 : (c + 1) * C2].astype(BF)
        for t in range(4):
            or1[t * C2 : (t + 1) * C2, :] = gr1[:, t * C : (t + 1) * C].astype(BF)
            or2[t * C2 : (t + 1) * C2, :] = gr2[:, t * C2 : (t + 1) * C2].astype(BF)
        os[...] = gs[...].astype(BF)
        obias[...] = jnp.sum(bsum[...], axis=1, keepdims=True)


def whole(shape, dtype=None):
    zeros = (0,) * len(shape)
    return pl.BlockSpec(shape, lambda i: zeros)


def once(shape):
    zeros = (0,) * len(shape)
    return pl.BlockSpec(shape, lambda i: zeros, pipeline_mode=pl.Buffered(1))


def image(shape):
    rest = (0,) * (len(shape) - 1)
    return pl.BlockSpec(shape, lambda i: (i,) + rest)


def run_forward(down_in, right_in, whole_v, cols):
    n = down_in.shape[0]
    sds = jax.ShapeDtypeStruct
    px = 1024
    kept = [(3, C2, px)] + [(LAYERS, C2, px)] * 5
    return pl.pallas_call(
        fwd_kernel,
        grid=(n,),
        in_specs=[image((1, 32, 32, C))] * 2 + [once(v.shape) for v in whole_v] + [once((1120, 4))],
        out_specs=[image((1, 32, 32, C))] * 2 + [image((1,) + s) for s in kept] + [whole((1120, 2))],
        out_shape=[sds((n, 32, 32, C), BF)] * 2 + [sds((n,) + s, BF) for s in kept] + [sds((1120, 2), F32)],
        scratch_shapes=[
            pltpu.VMEM((LAYERS, 2, 160, 960), BF),
            pltpu.VMEM((LAYERS, 2, 320, 960), BF),
            pltpu.VMEM((LAYERS, 160, 1280), BF),
            pltpu.VMEM((LAYERS, 160, 320), BF),
            pltpu.VMEM((LAYERS, 320, 1280), BF),
            pltpu.VMEM((960, 1152), BF),
            pltpu.VMEM((1280, 1024), BF),
            pltpu.VMEM((C, px), F32),
            pltpu.VMEM((C, px), F32),
        ],
        compiler_params=pltpu.CompilerParams(vmem_limit_bytes=60 << 20),
        name="forward",
    )(down_in, right_in, *whole_v, cols)


def run_backward(layer, down_g, right_g, cells_g, mask, kept, kappa, whole_v):
    n = down_g.shape[0]
    top = layer == 1
    sds = jax.ShapeDtypeStruct
    px = 1024
    shapes = [(1920, 160), (1920, 320), (1280, 160), (320, 160), (1280, 320)]
    flow = image((1, C, px))
    wide = image((1, C2, px))

    def pick(which):
        return pl.BlockSpec((1, 1, C2, px), lambda i: (i, which, 0, 0))

    def one_layer(shape):
        return pl.BlockSpec((1,) + shape, lambda i: (layer, 0, 0), pipeline_mode=pl.Buffered(1))

    cells = kept[0]
    ins = [down_g, right_g, mask] + ([] if top else [cells_g]) + [cells, cells] + list(kept[1:]) + [kappa] + list(whole_v)
    photo = image((1, 32, 32, C))
    in_specs = (
        ([photo] * 2 if top else [flow] * 2)
        + [image((1, 1, px))]
        + ([] if top else [wide])
        + [pick(layer), pick(layer + 1)]
        + [pick(layer)] * 5
        + [once((1120, 2))]
        + [one_layer(s) for s in shapes]
    )
    if top:
        out_specs = [flow, flow, wide]
        out_shape = [sds((n, C, px), F32)] * 2 + [sds((n, C2, px), F32)]
    else:
        out_specs = [photo] * 2
        out_shape = [sds((n, 32, 32, C), F32)] * 2
    return pl.pallas_call(
        functools.partial(bwd_kernel, top),
        grid=(n,),
        in_specs=in_specs,
        out_specs=out_specs + [once(s) for s in shapes] + [once((1120, 1))],
        out_shape=out_shape + [sds(s, BF) for s in shapes] + [sds((1120, 1), F32)],
        scratch_shapes=[
            pltpu.VMEM((2, 320, 480), BF),
            pltpu.VMEM((2, 320, 960), BF),
            pltpu.VMEM((320, 640), BF),
            pltpu.VMEM((320, 1280), BF),
            pltpu.VMEM((2, 320, 480), F32),
            pltpu.VMEM((2, 320, 960), F32),
            pltpu.VMEM((320, 640), F32),
            pltpu.VMEM((320, 160), F32),
            pltpu.VMEM((320, 1280), F32),
            pltpu.VMEM((1120, 128), F32),
            pltpu.VMEM((960, 1152), BF),
            pltpu.VMEM((480, 1152), BF),
            pltpu.VMEM((1280, 1024), BF),
            pltpu.VMEM((640, 1024), BF),
            pltpu.VMEM((160, 1024), BF),
            pltpu.VMEM((C, px), F32),
            pltpu.VMEM((C, px), F32),
        ],
        compiler_params=pltpu.CompilerParams(vmem_limit_bytes=60 << 20),
        name="backward%d" % layer,
    )(*ins)


def on_device(
    down_in,
    right_in,
    pixel_mask,
    down_cot,
    right_cot,
    v_down1,
    v_down2,
    v_right1,
    v_skip,
    v_right2,
    gains,
    biases,
):
    shards = (v_down1, v_down2, v_right1, v_skip, v_right2)
    whole_v = tuple(lax.all_gather(v, "dp", axis=1, tiled=True) for v in shards)
    cols = jnp.concatenate([gains, biases], axis=0).T
    n = down_in.shape[0]
    down_out, right_out, *kept, kappa = run_forward(down_in, right_in, whole_v, cols)
    mask = pixel_mask.reshape(n, 4, 8, 32).transpose(0, 2, 1, 3).reshape(n, 1, 1024).astype(F32)
    down_g, right_g, cells_g, *upper = run_backward(1, down_cot, right_cot, None, mask, kept, kappa, whole_v)
    down_grad, right_grad, *lower = run_backward(0, down_g, right_g, cells_g, mask, kept, kappa, whole_v)
    bias_sum = lax.psum(jnp.stack([lower[5][:, 0], upper[5][:, 0]]), ("dp", "grp"))
    sums = []
    for m in range(5):
        both = jnp.stack([lower[m], upper[m]])
        part = lax.psum_scatter(both, "dp", scatter_dimension=1, tiled=True)
        sums.append(lax.psum(part, "grp").astype(F32))
    units = []
    inverse = []
    for m in range(5):
        vals = whole_v[m].astype(F32)
        inv = lax.rsqrt(jnp.sum(vals * vals, axis=1))
        inverse.append(inv)
        units.append(shards[m].astype(F32) * inv[:, None, :])
    dots = jnp.concatenate([jnp.sum(units[m] * sums[m], axis=1) for m in range(5)], axis=1)
    dots = lax.psum(dots, "dp")
    grads = [
        sums[m] - units[m] * dots[:, None, lo:hi] for m, (lo, hi) in enumerate(SPANS)
    ]
    grad_gains = dots / (gains * jnp.concatenate(inverse, axis=1))
    return (down_out, right_out, down_grad, right_grad, *grads, grad_gains, bias_sum)


def solution(mesh):
    photo = P(("dp", "grp"), None, None, None)
    rows = P(None, "dp", None)
    return jax.shard_map(
        on_device,
        mesh=mesh,
        in_specs=(photo, photo, P(("dp", "grp"), None, None), photo, photo) + (rows,) * 5 + (P(), P()),
        out_specs=(photo,) * 4 + (rows,) * 5 + (P(), P()),
        check_vma=False,
    )
```

time: 1100 us -> 754 us (0.69)
  waiting for transfers between devices: 40.8 us -> 417 us
  matrix products: 364 us -> 0 us
  blocking collectives: 354 us -> 146 us
  other arithmetic: 207 us -> 23.4 us
  Pallas kernels: 0 us -> 125 us
  local copies, waits for them, and re-layouts: 110 us -> 13.8 us
    dot_general x126 -> x0, matrix products: 364 us -> none  [the longest x40 132 us: conv_input_grad(): jnp.einsum('bhwo,co->bhwc', grad_out, weight_tap, preferred_element_type=...]
    reduce_scatter x0 -> x4, waiting for transfers between devices: none -> 256 us  [on_device(): part = lax.psum_scatter(both, 'dp', scatter_dimension=1, tiled=True)]
    unnamed x1 -> x0, blocking collectives: 212 us -> none
    pallas_call x0 -> x3, Pallas kernels: none -> 125 us  [the longest x2 78.7 us: run_backward(): pl.pallas_call(functools.partial(bwd_kernel, top), grid=(n,), in_specs=in...]
    add x9 -> x0, other arithmetic: 81.4 us -> none  [the longest x7 73.9 us: conv_input_grad(): summed = placed if summed is None else summed + placed]
    all_gather x3, waiting for transfers between devices: 40 us -> 99.5 us  [on_device(): lax.all_gather(v, 'dp', axis=1, tiled=True)]
    unnamed x285 -> x56, local copies, waits for them, and re-layouts: 65.9 us -> 11.6 us
    unnamed x10, waiting for transfers between devices: 0.82 us -> 35.1 us
  transfers between devices with their start and end apart: 7 -> 9, of which waited for: 1 -> 8; matrix products, arithmetic and copies ran while one was open for 25% -> 3% of each run, Pallas kernels for 0% -> 0%
where the time goes in v1:
time: 754 us; the launch traced here: 741 us
  waiting for transfers between devices  417 us (55%)
  blocking collectives  146 us (19%)
  Pallas kernels  125 us (17%)
  other arithmetic  23.4 us (3%)
  between operations  15.1 us (2%)
  local copies, waits for them, and re-layouts  13.8 us (2%)
    reduce_scatter x4, waiting for transfers between devices, on_device(): part = lax.psum_scatter(both, 'dp', scatter_dimension=1, tiled=True)  256 us
    all_gather x3, waiting for transfers between devices, on_device(): lax.all_gather(v, 'dp', axis=1, tiled=True)  99.5 us
    pallas_call x2, Pallas kernels, run_backward(): pl.pallas_call(functools.partial(bwd_kernel, top), grid=(n,), in_specs=in...  78.7 us
    all_gather x2, blocking collectives, on_device(): lax.all_gather(v, 'dp', axis=1, tiled=True)  73.8 us
    pallas_call x1, Pallas kernels, run_forward(): pl.pallas_call(fwd_kernel, grid=(n,), in_specs=[image((1, 32, 32, C))] *...  46 us
    psum x1, blocking collectives, on_device(): lax.psum(jnp.stack([lower[5][:, 0], upper[5][:, 0]]), ('dp', 'grp'))  39.8 us
    unnamed x10, waiting for transfers between devices  35.1 us
    psum x1, waiting for transfers between devices, on_device(): sums.append(lax.psum(part, 'grp').astype(F32))  26.5 us
  transfers between devices with their start and end apart: 9, of which 8 were waited for; matrix products, arithmetic and copies ran while one was open for 3% of the time, Pallas kernels for 0%

profile of v1, /device:TPU:0, one launch (start us, length us, event | category | flops | bytes accessed | tf_op | source)
XLA Modules:
  0.0 741.2 jit_solution(10698018102484010052)
XLA Ops:
  7.2 0.0 all-gather.4.cloned.1.call-start
  7.3 1.8 copy.41
  9.1 0.0 all-gather.8.cloned.1.call-start
  9.2 0.7 all-gather.8.cloned.1.call-update
  9.9 0.0 all-gather.6.cloned.1.call-start
  9.9 1.9 copy.42
  11.8 0.0 reduce-scatter.10.cloned.1.call-start
  11.9 1.1 copy.43
  13.0 0.7 convert_element_type.57.mask
  13.7 35.6 %all_gather.18.vs.refs_11_.refs_12_ = bf16[2,320,160]{2,1,0:T(8,128)(2,1)} all-gather(bf16[2,40,160]{2,1,0:T(8,128)(2,1)S(1)} %copy-done.18), channel_id=1, replica_groups=mesh['dp'=8,'grp'=4] {'dp'}, dimensions={1}, use_global_device_ids=true | all-gather | bytes 230400 | tf_op jit(solution)/shard_map/all_gather | solution.py:504
  49.3 38.2 %all_gather.17.r1.refs_10_.refs_11_ = bf16[2,1280,160]{2,1,0:T(8,128)(2,1)} all-gather(bf16[2,160,160]{2,1,0:T(8,128)(2,1)S(1)} %copy-done.10), channel_id=1, replica_groups=mesh['dp'=8,'grp'=4] {'dp'}, dimensions={1}, use_global_device_ids=true | all-gather | bytes 921600 | tf_op jit(solution)/shard_map/all_gather | solution.py:504
  87.5 39.1 %all-gather.8.cloned.1.call-done.r2.refs_12_.refs_13_ = bf16[2,1280,320]{2,1,0:T(8,128)(2,1)} async-done(((bf16[2,160,320]{2,1,0:T(8,128)(2,1)}), bf16[2,1280,320]{2,1,0:T(8,128)(2,1)}) %all-gather.8.cloned.1.call-update) | async-done | bytes 1638416 | tf_op jit(solution)/shard_map/all_gather | solution.py:504
  126.6 60.4 %all-gather.6.cloned.1.call-done.v2.refs_9_.refs_10_ = bf16[2,1920,320]{2,1,0:T(8,128)(2,1)} async-done(((bf16[2,240,320]{2,1,0:T(8,128)(2,1)}), bf16[2,1920,320]{2,1,0:T(8,128)(2,1)}) %all-gather.6.cloned.1.call-update) | async-done | bytes 2457616 | tf_op jit(solution)/shard_map/all_gather | solution.py:504
  187.0 46.0 %forward.1 = (bf16[3,32,32,160]{3,2,1,0:T(8,128)(2,1)}, bf16[3,32,32,160]{3,2,1,0:T(8,128)(2,1)}, bf16[3,3,320,1024]{3,2,1,0:T(8,128)(2,1)}, bf16[3,2,320,1024]{...) custom-call(bf16[3,32,32,160]{3,2,1,0:T(8,128)(2,1)} %down_in.1, ...), custom_call_target="tpu_custom_call" | custom-call | tf_op jit(solution)/shard_map/forward/pallas_call | solution.py:404
  233.0 38.8 %backward1.1 = (f32[3,160,1024]{2,1,0:T(8,128)}, f32[3,160,1024]{2,1,0:T(8,128)}, f32[3,320,1024]{2,1,0:T(8,128)}, bf16[1920,160]{1,0:T(8,128)(2,1)}, bf16[1920,...) custom-call(bf16[3,32,32,160]{3,2,1,0:T(8,128)(2,1)} %down_g.1, ...), custom_call_target="tpu_custom_call" | custom-call | tf_op jit(solution)/shard_map/backward1/pallas_call | solution.py:459
  271.8 39.9 %backward0.1 = (f32[3,32,32,160]{3,2,1,0:T(8,128)}, f32[3,32,32,160]{3,2,1,0:T(8,128)}, bf16[1920,160]{1,0:T(8,128)(2,1)}, bf16[1920,320]{1,0:T(8,128)(2,1)}, bf...) custom-call(f32[3,160,1024]{2,1,0:T(8,128)} %get-tuple-element.46.down_g, ...), custom_call_target="tpu_custom_call" | custom-call | tf_op jit(solution)/shard_map/backward0/pallas_call | solution.py:459
  311.7 2.6 pad_maximum_fusion.3
  314.3 0.0 reduce-scatter.6.cloned.1.call-start
  314.3 1.7 pad_maximum_fusion.1
  316.0 0.0 reduce-scatter.12.cloned.1.call-start
  316.1 1.1 copy-done.13
  317.2 3.0 pad_maximum_fusion.2
  320.3 0.3 reduce-scatter.8.cloned.1.call-start
  320.5 1.1 copy-done.7
  321.6 2.2 pad_maximum_fusion
  323.8 0.0 all-reduce.5.cloned.1.call-start
  323.9 1.2 copy-done.1
  325.1 0.3 multiply_reduce_fusion.3
  325.5 1.1 multiply_reduce_fusion.4
  326.6 0.6 dynamic-slice
  327.9 0.5 multiply_reduce_fusion.2
  328.4 1.1 copy-done.3
  329.4 0.5 multiply_reduce_fusion.1
  329.9 0.8 pad_maximum_fusion.4
  330.7 0.0 all-reduce.7.cloned.1.call-start
  330.8 0.7 multiply_reduce_fusion
  331.5 1.4 reduce.1
  332.9 1.3 reduce
  334.3 0.1 concatenate.11
  334.4 43.0 %reduce-scatter.10.cloned.1.call-done = bf16[2,160,160]{2,1,0:T(8,128)(2,1)} async-done(((bf16[2,1280,160]{2,1,0:T(8,128)(2,1)}), bf16[2,160,160]{2,1,0:T(8,128)(2,1)}) %reduce-scatter.10.cloned.1.call-update) | async-done | bytes 102416 | tf_op jit(solution)/shard_map/reduce_scatter | solution.py:515
  377.4 69.1 %reduce-scatter.6.cloned.1.call-done = bf16[2,240,160]{2,1,0:T(8,128)(2,1)} async-done(((bf16[2,1920,160]{2,1,0:T(8,128)(2,1)}), bf16[2,240,160]{2,1,0:T(8,128)(2,1)}) %reduce-scatter.6.cloned.1.call-update) | async-done | bytes 153616 | tf_op jit(solution)/shard_map/reduce_scatter | solution.py:515
  446.5 69.4 %reduce-scatter.12.cloned.1.call-done = bf16[2,160,320]{2,1,0:T(8,128)(2,1)} async-done(((bf16[2,1280,320]{2,1,0:T(8,128)(2,1)}), bf16[2,160,320]{2,1,0:T(8,128)(2,1)}) %reduce-scatter.12.cloned.1.call-update) | async-done | bytes 204816 | tf_op jit(solution)/shard_map/reduce_scatter | solution.py:515
  515.9 74.5 %reduce-scatter.8.cloned.1.call-done = bf16[2,240,320]{2,1,0:T(8,128)(2,1)} async-done(((bf16[2,1920,320]{2,1,0:T(8,128)(2,1)}), bf16[2,240,320]{2,1,0:T(8,128)(2,1)}) %reduce-scatter.8.cloned.1.call-update) | async-done | bytes 307216 | tf_op jit(solution)/shard_map/reduce_scatter | solution.py:515
  590.4 39.8 %psum.55 = f32[2,1120]{1,0:T(2,128)} all-reduce(f32[2,1120]{1,0:T(2,128)S(1)} %pad_maximum_fusion.6), channel_id=1, replica_groups=mesh['dp'=8,'grp'=4] {'dp','grp'}, use_global_device_ids=true, to_apply=%region_21.0 | all-reduce | flops 2240 | bytes 17920 | tf_op jit(solution)/shard_map/psum | solution.py:511
  630.2 34.3 %all-reduce.5.cloned.1.call-done = bf16[2,320,160]{2,1,0:T(8,128)(2,1)} async-done(((bf16[2,320,160]{2,1,0:T(8,128)(2,1)}), bf16[2,320,160]{2,1,0:T(8,128)(2,1)}) %all-reduce.5.cloned.1.call-update) | async-done | bytes 204816
  664.5 0.8 constant_dynamic-slice_fusion
  665.3 11.1 %psum.52 = bf16[2,40,160]{2,1,0:T(8,128)(2,1)S(1)} all-reduce(bf16[2,40,160]{2,1,0:T(8,128)(2,1)S(1)} %constant_dynamic-slice_fusion), channel_id=1, replica_groups=mesh['dp'=8,'grp'=4] {'grp'}, use_global_device_ids=true, to_apply=%region_14.0 | all-reduce | flops 12800 | bytes 51200 | tf_op jit(solution)/shard_map/psum | solution.py:516
  676.4 26.5 %all-reduce.7.cloned.1.call-done = (bf16[2,240,160]{2,1,0:T(8,128)(2,1)}, bf16[2,240,320]{2,1,0:T(8,128)(2,1)}, bf16[2,160,160]{2,1,0:T(8,128)(2,1)}, bf16[2,160,320]{2,1,0:T(8,128)(2,1)}) async-done(((bf16[2,240,160]{2,1,0:T(8,128)(2,1)}, bf16[2,240,320]{2,1,0:T(8,128)(2,1)}, bf16[2,160,160]{2,1,0:T(8,128)(2,1)}, bf16[2,160,320]{2,1,0:T(8,128)(2,1)}), (bf16[2,240,160]{2,1,0:T(8,128)(2,1)}, ...) | async-done | bytes 768016 | tf_op jit(solution)/shard_map/psum | solution.py:516
  702.9 1.1 fusion.1
  704.0 1.1 fusion
  705.1 1.0 fusion.3
  706.1 1.0 fusion.2
  707.2 0.1 concatenate.10
  707.3 21.8 %psum.54 = f32[2,1120]{1,0:T(2,128)S(1)} all-reduce(f32[2,1120]{1,0:T(2,128)S(1)} %concatenate.10), channel_id=1, replica_groups=mesh['dp'=8,'grp'=4] {'dp'}, use_global_device_ids=true, to_apply=%region_20.0 | all-reduce | flops 2240 | bytes 17920 | tf_op jit(solution)/shard_map/psum | solution.py:525
  729.1 0.1 fusion.6
  729.2 0.1 fusion.5
  729.3 0.1 convert_subtract_fusion.2
  729.4 0.9 copy.47
  730.3 0.1 convert_subtract_fusion
  730.4 1.1 copy.48
  731.5 0.8 convert_subtract_fusion.3
  732.3 0.7 convert_subtract_fusion.4
  732.9 0.9 convert_subtract_fusion.1
  733.8 0.6 multiply_divide_fusion
  (67 shorter events, 0.4 us)
Async XLA Ops:
  7.2 4.7 copy-start.23
  7.2 4.7 copy-start.22
  7.2 5.8 copy-start.21
  7.2 6.5 copy-start.18
  7.2 42.0 %copy-start.10 = (bf16[2,160,160]{2,1,0:T(8,128)(2,1)S(1)}, bf16[2,160,160]{2,1,0:T(8,128)(2,1)}, u32[]{:S(2)}) copy-start(bf16[2,160,160]{2,1,0:T(8,128)(2,1)} %param.19) | copy-start | bytes 307204
  7.2 80.2 %all-gather.4.cloned.1.call-start = ((), (), s32[]{:S(2)}) async-start(), calls=%async_computation.4 | async-start | bytes 2211840 | tf_op jit(solution)/shard_map/all_gather | solution.py:504
  9.1 117.5 %all-gather.8.cloned.1.call-start = ((), (), s32[]{:S(2)}) async-start(), calls=%async_computation.6 | async-start | bytes 2211840 | tf_op jit(solution)/shard_map/all_gather | solution.py:504
  9.9 177.1 %all-gather.6.cloned.1.call-start = ((), (), s32[]{:S(2)}) async-start(), calls=%async_computation.5 | async-start | bytes 3317760 | tf_op jit(solution)/shard_map/all_gather | solution.py:504
  11.8 365.5 %reduce-scatter.10.cloned.1.call-start = ((), (), s32[]{:S(2)}) async-start(), calls=%async_computation.9 | async-start | bytes 1474560 | tf_op jit(solution)/shard_map/reduce_scatter | solution.py:515
  271.8 39.9 %copy-start.16 = (bf16[1280,160]{1,0:T(8,128)(2,1)S(1)}, bf16[1280,160]{1,0:T(8,128)(2,1)}, u32[]{:S(2)}) copy-start(bf16[1280,160]{1,0:T(8,128)(2,1)} %get-tuple-element.56) | copy-start | bytes 1228804
  311.7 2.7 copy-start.14
  311.7 2.7 copy-start.15
  314.3 132.2 %reduce-scatter.6.cloned.1.call-start = ((), (), s32[]{:S(2)}) async-start(), calls=%async_computation.7 | async-start | bytes 2211840 | tf_op jit(solution)/shard_map/reduce_scatter | solution.py:515
  316.0 1.2 copy-start.13
  316.0 199.8 %reduce-scatter.12.cloned.1.call-start = ((), (), s32[]{:S(2)}) async-start(), calls=%async_computation.10 | async-start | bytes 2211840 | tf_op jit(solution)/shard_map/reduce_scatter | solution.py:515
  317.2 3.3 copy-start.8
  320.2 1.4 copy-start.7
  320.3 270.1 %reduce-scatter.8.cloned.1.call-start = ((), (), s32[]{:S(2)}) async-start(), calls=%async_computation.8 | async-start | bytes 3317760 | tf_op jit(solution)/shard_map/reduce_scatter | solution.py:515
  323.8 1.3 copy-start.1
  323.8 2.8 copy-start.24
  323.8 4.0 copy-start.2
  323.8 340.7 %all-reduce.5.cloned.1.call-start = ((), (), s32[]{:S(2)}) async-start(), calls=%async_computation.11 | async-start | bytes 655360
  325.4 4.5 copy-start.19
  325.4 4.5 copy-start.20
  327.8 1.6 copy-start.3
  328.3 2.4 copy-start
  330.7 372.1 %all-reduce.7.cloned.1.call-start = ((), (), s32[]{:S(2)}) async-start(), calls=%async_computation.12 | async-start | bytes 2048000 | tf_op jit(solution)/shard_map/psum | solution.py:516
  331.5 371.4 %copy-start.5 = (bf16[2,240,160]{2,1,0:T(8,128)(2,1)S(1)}, bf16[2,240,160]{2,1,0:T(8,128)(2,1)}, u32[]{:S(2)}) copy-start(bf16[2,240,160]{2,1,0:T(8,128)(2,1)} %copy.41) | copy-start | bytes 460804
  331.5 372.5 %copy-start.4 = (bf16[2,240,320]{2,1,0:T(8,128)(2,1)S(1)}, bf16[2,240,320]{2,1,0:T(8,128)(2,1)}, u32[]{:S(2)}) copy-start(bf16[2,240,320]{2,1,0:T(8,128)(2,1)} %copy.42) | copy-start | bytes 921604
  331.5 374.6 %copy-start.6 = (bf16[2,160,320]{2,1,0:T(8,128)(2,1)S(1)}, bf16[2,160,320]{2,1,0:T(8,128)(2,1)}, u32[]{:S(2)}) copy-start(bf16[2,160,320]{2,1,0:T(8,128)(2,1)} %param.21) | copy-start | bytes 614404
  702.9 26.4 %copy-start.12 = (bf16[2,240,160]{2,1,0:T(8,128)(2,1)S(1)}, bf16[2,240,160]{2,1,0:T(8,128)(2,1)}, u32[]{:S(2)}) copy-start(bf16[2,240,160]{2,1,0:T(8,128)(2,1)} %get-tuple-element.96) | copy-start | bytes 460804
  702.9 27.4 %copy-start.9 = (bf16[2,240,320]{2,1,0:T(8,128)(2,1)S(1)}, bf16[2,240,320]{2,1,0:T(8,128)(2,1)}, u32[]{:S(2)}) copy-start(bf16[2,240,320]{2,1,0:T(8,128)(2,1)} %get-tuple-element.97) | copy-start | bytes 921604
  729.4 2.1 copy-start.17
  730.3 2.7 copy-start.11
Sparse Core Ops, SparseCore 0:
  10.8 66.0 all-gather.3
  79.1 47.4 all-gather.7
  129.4 57.4 all-gather.5
  314.4 62.9 reduce-scatter.9
  380.7 65.7 reduce-scatter.5
  450.2 65.6 reduce-scatter.11
  519.6 70.7 reduce-scatter.7
  594.3 70.1 all-reduce.4
  667.3 35.5 all-reduce.6
